TPU v7x, 512 devices: a whole 4x4x16 slice. The times are simulated.
512 devices in a mesh: wide: 32 (over z, core), narrow: 16 (over y, x).
Axes of the slice: x: 4, y: 4, z: 16, core: 2. Of those that a mesh axis runs over, the one named last changes fastest.
Arguments:
- hidden: bfloat16 [2048, 2048], P('wide'), may hold values from -6 to 6
- attn_gain: float32 [2048], replicated, may hold values from 0.1 to 1.9
- expert_gain: float32 [2048], replicated, may hold values from 0.1 to 1.9
- query_weight: bfloat16 [2048, 2048], P('wide', 'narrow'), may hold values from -0.125 to 0.125
- key_weight: bfloat16 [2048, 2048], P('wide', 'narrow'), may hold values from -0.125 to 0.125
- value_weight: bfloat16 [2048, 2048], P('wide', 'narrow'), may hold values from -0.125 to 0.125
- output_weight: bfloat16 [2048, 2048], P('wide', 'narrow'), may hold values from -0.125 to 0.125
- router_weight: bfloat16 [2048, 64], replicated, may hold values from -0.125 to 0.125
- gate_weight: bfloat16 [64, 2048, 1024], P('wide', None, 'narrow'), may hold values from -0.125 to 0.125
- up_weight: bfloat16 [64, 2048, 1024], P('wide', None, 'narrow'), may hold values from -0.125 to 0.125
- down_weight: bfloat16 [64, 1024, 2048], P('wide', 'narrow'), may hold values from -0.1875 to 0.1875
- prefix_keys: bfloat16 [256, 8, 2048], P('wide', None, 'narrow'), may hold values from -6 to 6
- prefix_values: bfloat16 [256, 8, 2048], P('wide', None, 'narrow'), may hold values from -6 to 6
- cache_keys: bfloat16 [32, 1024, 2048], P('wide', None, 'narrow'), may hold values from -256 to 256
- cache_values: bfloat16 [32, 1024, 2048], P('wide', None, 'narrow'), may hold values from -6 to 6
- parents: int32 [32, 64], P('wide'), may hold values from 0 to 62, as said below
- cache_lengths: int32 [32], P('wide'), may hold values from 1 to 960, 15360 in all
- group_ids: int32 [32], replicated, may hold values from 0 to 7
- expert_ids: int32 [2048, 8], P('wide'), may hold values from 0 to 63, all different within a row; in each aligned block of 64 rows (0 to 63, 64 to 127, ...) at most 9 rows name the same one
- accepted: int32 [32], P('wide'), may hold values from 0 to 63
Outputs:
- layer_out: bfloat16 [2048, 2048], P('wide', 'narrow')
- new_keys: bfloat16 [32, 1024, 2048], P('wide', None, 'narrow')
- new_values: bfloat16 [32, 1024, 2048], P('wide', None, 'narrow')
Inputs may be any that keep to these rules, and one draw needn't show every extreme that they name: `parents`: node 0 of each tree is the root and its own parent; node i > 0 has its parent among nodes max(0, i - 4) to i - 1; the parent of node 63 is node 62. `expert_ids`: the 8 experts of a token differ; among the tokens of one index of wide no expert is named more than 9 times, a bound that some block reaches in some of them.
All inputs are finite; a program needn't handle non-finite values. No bound on the sum of `cache_lengths` on one device may be relied on, other than what follows from the above.
Results may differ from a plain program's by a relative error of at most 0.01.
The roundings to bfloat16 on the way count: a program that leaves them out, or rounds other values in their place, can miss the bound.
Values may be sent and summed in bfloat16 or wider, within the bound.
A program may use at most 64 MiB of HBM per device.

v0:
```python
import math
import jax
import jax.numpy as jnp
from jax import lax
from jax.sharding import PartitionSpec as P

HD = 128
E = 64
SINK = 4
WIN = 512
CAP = 9
norm_eps = 1e-06


def rms_scale(rows, row_gain):
    widened = rows.astype(jnp.float32)
    power_mean = jnp.mean(widened * widened, axis=-1, keepdims=True)
    return (widened * lax.rsqrt(power_mean + norm_eps) * row_gain).astype(jnp.bfloat16)


def tree_links(parents):
    tree_size = parents.shape[-1]
    node_ids = jnp.arange(tree_size, dtype=jnp.int32)
    linked = (node_ids[:, None] == node_ids[None, :]) | (parents[..., :, None] == node_ids)
    jumper = parents
    for doubling in range(tree_size.bit_length()):
        hop_table = (jumper[..., :, None] == node_ids).astype(jnp.float32)
        through = jnp.einsum(
            "...ij,...jk->...ik",
            hop_table,
            linked.astype(jnp.float32),
            precision=lax.Precision.HIGHEST,
        )
        linked = linked | (through > 0.5)
        jumper = jnp.take_along_axis(jumper, jumper, axis=-1)
    depths = jnp.sum(linked.astype(jnp.int32), axis=-1) - 1
    return (linked, depths)


def body(
    hidden,
    attn_gain,
    expert_gain,
    query_weight,
    key_weight,
    value_weight,
    output_weight,
    router_weight,
    gate_weight,
    up_weight,
    down_weight,
    prefix_keys,
    prefix_values,
    cache_keys,
    cache_values,
    parents,
    cache_lengths,
    group_ids,
    expert_ids,
    accepted,
):
    tok_count, model_width = hidden.shape
    req_count, tree_size = parents.shape
    cache_size = cache_keys.shape[1]
    local_width = query_weight.shape[1]
    head_size = HD
    head_count = local_width // head_size
    group_count = prefix_keys.shape[1]
    narrow_count = lax.axis_size("narrow")
    wide_count = lax.axis_size("wide")
    slice_width = model_width // narrow_count
    narrow_pos = lax.axis_index("narrow")
    wide_pos = lax.axis_index("wide")
    scale_factor = 1.0 / math.sqrt(head_size)
    normed = rms_scale(hidden, attn_gain)
    own_groups = lax.dynamic_slice_in_dim(group_ids, wide_pos * req_count, req_count)
    gathered = (
        lax.all_gather(query_weight, "wide", axis=0, tiled=True),
        lax.all_gather(key_weight, "wide", axis=0, tiled=True),
        lax.all_gather(value_weight, "wide", axis=0, tiled=True),
        lax.all_gather(output_weight, "wide", axis=0, tiled=True),
        lax.all_gather(prefix_keys, "wide", axis=0, tiled=True),
        lax.all_gather(prefix_values, "wide", axis=0, tiled=True),
    )
    query_full, key_full, value_full, output_full, shared_keys, shared_values = gathered
    prefix_len = shared_keys.shape[0]
    group_keys = jnp.take(
        shared_keys.reshape(prefix_len, group_count, head_count, head_size), own_groups, axis=1
    )
    group_values = jnp.take(
        shared_values.reshape(prefix_len, group_count, head_count, head_size), own_groups, axis=1
    )
    queries = jnp.dot(normed, query_full, preferred_element_type=jnp.float32).astype(jnp.bfloat16)
    keys_new = jnp.dot(normed, key_full, preferred_element_type=jnp.float32).astype(jnp.bfloat16)
    values_new = jnp.dot(normed, value_full, preferred_element_type=jnp.float32).astype(
        jnp.bfloat16
    )
    block_shape = (req_count, tree_size, head_count, head_size)
    query_blocks = queries.reshape(block_shape)
    key_blocks = keys_new.reshape(block_shape)
    value_blocks = values_new.reshape(block_shape)
    own_keys = cache_keys.reshape(req_count, cache_size, head_count, head_size)
    own_values = cache_values.reshape(req_count, cache_size, head_count, head_size)
    slot_ids = jnp.arange(cache_size, dtype=jnp.int32)
    lengths = cache_lengths[:, None]
    cache_mask = (slot_ids < lengths) & ((slot_ids < SINK) | (slot_ids >= lengths - WIN))
    ancestry, depths = tree_links(parents)
    cache_allowed = cache_mask[:, None, None, :]
    tree_allowed = ancestry[:, None, :, :]
    prefix_scores = (
        jnp.einsum("rqhd,prhd->rhqp", query_blocks, group_keys, preferred_element_type=jnp.float32)
        * scale_factor
    )
    cache_scores = (
        jnp.einsum("rqhd,rkhd->rhqk", query_blocks, own_keys, preferred_element_type=jnp.float32)
        * scale_factor
    )
    tree_scores = (
        jnp.einsum("rqhd,rkhd->rhqk", query_blocks, key_blocks, preferred_element_type=jnp.float32)
        * scale_factor
    )
    row_top = jnp.maximum(
        jnp.max(prefix_scores, axis=-1),
        jnp.maximum(
            jnp.max(jnp.where(cache_allowed, cache_scores, -jnp.inf), axis=-1),
            jnp.max(jnp.where(tree_allowed, tree_scores, -jnp.inf), axis=-1),
        ),
    )[..., None]
    prefix_weights = jnp.exp(prefix_scores - row_top)
    cache_weights = jnp.where(cache_allowed, jnp.exp(cache_scores - row_top), 0.0)
    tree_weights = jnp.where(tree_allowed, jnp.exp(tree_scores - row_top), 0.0)
    row_total = (
        jnp.sum(prefix_weights, axis=-1)
        + jnp.sum(cache_weights, axis=-1)
        + jnp.sum(tree_weights, axis=-1)
    )
    weighted = jnp.einsum(
        "rhqp,prhd->rqhd",
        prefix_weights.astype(jnp.bfloat16),
        group_values,
        preferred_element_type=jnp.float32,
    )
    weighted = weighted + jnp.einsum(
        "rhqk,rkhd->rqhd",
        cache_weights.astype(jnp.bfloat16),
        own_values,
        preferred_element_type=jnp.float32,
    )
    weighted = weighted + jnp.einsum(
        "rhqk,rkhd->rqhd",
        tree_weights.astype(jnp.bfloat16),
        value_blocks,
        preferred_element_type=jnp.float32,
    )
    attended = (
        (weighted / jnp.transpose(row_total, (0, 2, 1))[..., None])
        .astype(jnp.bfloat16)
        .reshape(tok_count, local_width)
    )
    partial_value = lax.dot_general(
        attended, output_full, (((1,), (1,)), ((), ())), preferred_element_type=jnp.float32
    )
    summed = lax.psum(partial_value, "narrow")
    mixed = (hidden.astype(jnp.float32) + summed).astype(jnp.bfloat16)
    mixed_part = lax.dynamic_slice_in_dim(mixed, narrow_pos * slice_width, slice_width, 1)
    normed_moe = rms_scale(mixed, expert_gain)
    logits = jnp.dot(normed_moe, router_weight, preferred_element_type=jnp.float32)
    expert_range = jnp.arange(E, dtype=jnp.int32)
    top_count = expert_ids.shape[1]
    matches = expert_ids[:, :, None] == expert_range
    chosen = jnp.sum(jnp.where(matches, logits[:, None, :], 0.0), axis=-1)
    shares = jax.nn.softmax(chosen, axis=-1)
    flat_experts = expert_ids.reshape(-1)
    expert_table = (flat_experts[:, None] == expert_range).astype(jnp.int32)
    earlier = jnp.cumsum(expert_table, axis=0) - expert_table
    slot_ranks = jnp.sum(earlier * expert_table, axis=1)
    targets = flat_experts * CAP + slot_ranks
    repeated = jnp.broadcast_to(
        normed_moe[:, None, :], (tok_count, top_count, model_width)
    ).reshape(tok_count * top_count, model_width)
    exp_local = gate_weight.shape[0]
    send_rows = jnp.zeros((E * CAP, model_width), jnp.bfloat16).at[targets].set(repeated)
    send_rows = send_rows.reshape(wide_count, exp_local, CAP, model_width)
    routed = lax.all_to_all(send_rows, "wide", split_axis=0, concat_axis=0, tiled=True)
    gate_out = jnp.einsum("secd,edf->secf", routed, gate_weight, preferred_element_type=jnp.float32)
    up_out = jnp.einsum("secd,edf->secf", routed, up_weight, preferred_element_type=jnp.float32)
    activated = (jax.nn.silu(gate_out) * up_out).astype(jnp.bfloat16)
    produced = jnp.einsum(
        "secf,efd->secd", activated, down_weight, preferred_element_type=jnp.float32
    ).astype(jnp.bfloat16)
    returned = lax.all_to_all(produced, "wide", split_axis=0, concat_axis=0, tiled=True)
    fetched = returned.reshape(E * CAP, model_width)[targets].reshape(
        tok_count, top_count, model_width
    )
    partial_moe = jnp.sum(shares[:, :, None] * fetched.astype(jnp.float32), axis=1)
    moe_part = lax.psum_scatter(partial_moe, "narrow", scatter_dimension=1, tiled=True)
    layer_out = (mixed_part.astype(jnp.float32) + moe_part).astype(jnp.bfloat16)
    on_path = jnp.take_along_axis(ancestry, accepted[:, None, None], axis=1)[:, 0, :]
    slots = jnp.where(on_path, cache_lengths[:, None] + depths, cache_size)
    request_rows = jnp.broadcast_to(
        jnp.arange(req_count, dtype=jnp.int32)[:, None], (req_count, tree_size)
    )
    new_keys = cache_keys.at[request_rows, slots].set(
        keys_new.reshape(req_count, tree_size, local_width), mode="drop"
    )
    new_values = cache_values.at[request_rows, slots].set(
        values_new.reshape(req_count, tree_size, local_width), mode="drop"
    )
    return (layer_out, new_keys, new_values)


def solution(mesh):
    in_specs = (
        P("wide", None),
        P(),
        P(),
        P("wide", "narrow"),
        P("wide", "narrow"),
        P("wide", "narrow"),
        P("wide", "narrow"),
        P(),
        P("wide", None, "narrow"),
        P("wide", None, "narrow"),
        P("wide", "narrow", None),
        P("wide", None, "narrow"),
        P("wide", None, "narrow"),
        P("wide", None, "narrow"),
        P("wide", None, "narrow"),
        P("wide", None),
        P("wide"),
        P(),
        P("wide", None),
        P("wide"),
    )
    out_specs = (P("wide", "narrow"), P("wide", None, "narrow"), P("wide", None, "narrow"))
    return jax.shard_map(body, mesh=mesh, in_specs=in_specs, out_specs=out_specs, check_vma=False)
```

profile of v0, /device:TPU:2, one launch (start us, length us, event | category | flops | bytes accessed | tf_op | source)
XLA Modules:
  0.0 689.3 jit_solution(3292197298421425880)
XLA Ops:
  7.2 1.0 copy.120
  8.2 1.1 copy.121
  9.9 1.2 dynamic_slice.6
  13.8 1.1 fusion.39
  14.9 1.0 fusion.30
  15.9 1.4 gather_fusion.1
  23.1 37.7 %all_gather.18 = bf16[256,8,128]{2,0,1:T(8,128)(2,1)S(1)} all-gather(bf16[8,8,128]{2,0,1:T(8,128)(2,1)S(1)} %copy.59), channel_id=1, replica_groups=mesh['wide'=32,'narrow'=16] {'wide'}, dimensions={0}, use_global_device_ids=true | all-gather | bytes 540672 | tf_op jit(solution)/shard_map/all_gather | solution.py:83
  60.8 28.5 %all_gather.20 = bf16[256,8,128]{2,0,1:T(8,128)(2,1)S(1)} all-gather(bf16[8,8,128]{2,0,1:T(8,128)(2,1)S(1)} %copy.60), channel_id=1, replica_groups=mesh['wide'=32,'narrow'=16] {'wide'}, dimensions={0}, use_global_device_ids=true | all-gather | bytes 540672 | tf_op jit(solution)/shard_map/all_gather | solution.py:82
  89.3 30.0 %all_gather.19 = bf16[2048,128]{1,0:T(8,128)(2,1)S(1)} all-gather(bf16[64,128]{1,0:T(8,128)(2,1)S(1)} %copy-done.7), channel_id=1, replica_groups=mesh['wide'=32,'narrow'=16] {'wide'}, dimensions={0}, use_global_device_ids=true | all-gather | bytes 540672 | tf_op jit(solution)/shard_map/all_gather | solution.py:78
  119.2 28.5 %all_gather.21 = bf16[2048,128]{1,0:T(8,128)(2,1)S(1)} all-gather(bf16[64,128]{1,0:T(8,128)(2,1)S(1)} %copy-done.8), channel_id=1, replica_groups=mesh['wide'=32,'narrow'=16] {'wide'}, dimensions={0}, use_global_device_ids=true | all-gather | bytes 540672 | tf_op jit(solution)/shard_map/all_gather | solution.py:79
  150.2 29.9 %all_gather.22 = bf16[2048,128]{1,0:T(8,128)(2,1)S(1)} all-gather(bf16[64,128]{1,0:T(8,128)(2,1)S(1)} %copy-done.9), channel_id=1, replica_groups=mesh['wide'=32,'narrow'=16] {'wide'}, dimensions={0}, use_global_device_ids=true | all-gather | bytes 540672 | tf_op jit(solution)/shard_map/all_gather | solution.py:80
  180.4 28.5 %all_gather.23 = bf16[2048,128]{1,0:T(8,128)(2,1)S(1)} all-gather(bf16[64,128]{1,0:T(8,128)(2,1)S(1)} %copy-done.10), channel_id=1, replica_groups=mesh['wide'=32,'narrow'=16] {'wide'}, dimensions={0}, use_global_device_ids=true | all-gather | bytes 540672 | tf_op jit(solution)/shard_map/all_gather | solution.py:81
  209.1 1.3 fusion.35
  210.9 1.2 reduce-window.6
  212.5 110.2 %all-reduce.3.cloned.1.call-done = f32[64,2048]{1,0:T(8,128)} async-done(((f32[64,2048]{1,0:T(8,128)}), f32[64,2048]{1,0:T(8,128)}) %all-reduce.3.cloned.1.call-update) | async-done | bytes 524304 | tf_op jit(solution)/shard_map/psum | solution.py:163
  322.8 1.2 fusion.36
  324.7 4.5 scatter_custom_fusion
  329.2 2.8 reshape.738
  332.0 4.8 copy.67
  336.9 125.1 %all_to_all.10 = bf16[32,2,9,2048]{3,1,2,0:T(2,128)(2,1)S(1)} all-to-all(bf16[32,2,9,2048]{3,1,2,0:T(2,128)(2,1)S(1)} %copy.67), channel_id=1, replica_groups=mesh['wide'=32,'narrow'=16] {'wide'}, dimensions={0} | all-to-all | bytes 4718592 | tf_op jit(solution)/shard_map/all_to_all | solution.py:184
  462.0 1.6 fusion.9
  463.6 4.1 fusion.1
  467.6 5.5 copy.70
  473.1 4.1 all-to-all-start.1
  477.5 1.2 fusion.127
  479.3 110.6 %all-to-all-done.1 = bf16[32,2,9,2048]{3,1,2,0:T(2,128)(2,1)S(1)} async-done(((bf16[32,2,9,2048]{3,1,2,0:T(2,128)(2,1)}), bf16[32,2,9,2048]{3,1,2,0:T(2,128)(2,1)S(1)}, u32[]{:S(2)}, u32[]{:S(2)}) %all-to-all-start.1) | async-done | bytes 2359328 | tf_op jit(solution)/shard_map/all_to_all | solution.py:191
  589.9 3.3 copy.71
  593.2 3.4 reshape.739
  596.6 3.3 gather_fusion
  599.9 4.2 fusion
  606.9 74.2 %reduce-scatter.2.cloned.1.call-done = f32[64,128]{1,0:T(8,128)} async-done(((f32[64,2048]{1,0:T(8,128)}), f32[64,128]{1,0:T(8,128)}) %reduce-scatter.2.cloned.1.call-update) | async-done | bytes 32784 | tf_op jit(solution)/shard_map/reduce_scatter | solution.py:196
  681.1 1.4 add_convert_fusion
  (104 shorter events, 13.8 us)
Async XLA Ops:
  7.2 456.4 %copy-start = (bf16[2,64,2048]{2,1,0:T(8,128)(2,1)S(1)}, bf16[2,64,2048]{2,1,0:T(8,128)(2,1)}, u32[]{:S(2)}) copy-start(bf16[2,64,2048]{2,1,0:T(8,128)(2,1)} %param.34) | copy-start | bytes 1572868
  7.2 315.6 %all-reduce.3.cloned.1.call-start = ((), (), s32[]{:S(2)}) async-start(), calls=%async_computation.3 | async-start | bytes 1048576 | tf_op jit(solution)/shard_map/psum | solution.py:163
  8.2 140.2 %copy-start.2 = (bf16[1,1024,128]{2,1,0:T(8,128)(2,1)}, bf16[1,1024,128]{2,1,0:T(8,128)(2,1)S(1)}, u32[]{:S(2)}) copy-start(bf16[1,1024,128]{2,1,0:T(8,128)(2,1)S(1)} %copy.120) | copy-start | bytes 786436
  8.2 14.8 %copy-start.12 = (bf16[8,8,128]{2,1,0:T(8,128)(2,1)S(1)}, bf16[8,8,128]{2,1,0:T(8,128)(2,1)}, u32[]{:S(2)}) copy-start(bf16[8,8,128]{2,1,0:T(8,128)(2,1)} %param.35) | copy-start | bytes 49156
  8.2 14.8 %copy-start.13 = (bf16[8,8,128]{2,1,0:T(8,128)(2,1)S(1)}, bf16[8,8,128]{2,1,0:T(8,128)(2,1)}, u32[]{:S(2)}) copy-start(bf16[8,8,128]{2,1,0:T(8,128)(2,1)} %param.36) | copy-start | bytes 49156
  15.9 73.4 %copy-start.7 = (bf16[64,128]{1,0:T(8,128)(2,1)S(1)}, bf16[64,128]{1,0:T(8,128)(2,1)}, u32[]{:S(2)}) copy-start(bf16[64,128]{1,0:T(8,128)(2,1)} %param.27) | copy-start | bytes 49156
  18.0 101.2 %copy-start.8 = (bf16[64,128]{1,0:T(8,128)(2,1)S(1)}, bf16[64,128]{1,0:T(8,128)(2,1)}, u32[]{:S(2)}) copy-start(bf16[64,128]{1,0:T(8,128)(2,1)} %param.28) | copy-start | bytes 49156
  18.8 128.9 %copy-start.6 = (bf16[64,2048]{1,0:T(8,128)(2,1)S(1)}, bf16[64,2048]{1,0:T(8,128)(2,1)}, u32[]{:S(2)}) copy-start(bf16[64,2048]{1,0:T(8,128)(2,1)} %param.24) | copy-start | bytes 786436
  18.8 128.9 %copy-start.16 = (f32[2048]{0:T(1024)S(1)}, f32[2048]{0:T(1024)}, u32[]{:S(2)}) copy-start(f32[2048]{0:T(1024)} %param.25) | copy-start | bytes 24580
  89.3 61.0 %copy-start.9 = (bf16[64,128]{1,0:T(8,128)(2,1)S(1)}, bf16[64,128]{1,0:T(8,128)(2,1)}, u32[]{:S(2)}) copy-start(bf16[64,128]{1,0:T(8,128)(2,1)} %param.29) | copy-start | bytes 49156
  147.7 32.6 %copy-start.10 = (bf16[64,128]{1,0:T(8,128)(2,1)S(1)}, bf16[64,128]{1,0:T(8,128)(2,1)}, u32[]{:S(2)}) copy-start(bf16[64,128]{1,0:T(8,128)(2,1)} %param.30) | copy-start | bytes 49156
  149.3 61.1 %copy-start.11 = (s32[64,8]{0,1:T(8,128)S(1)}, s32[64,8]{0,1:T(8,128)}, u32[]{:S(2)}) copy-start(s32[64,8]{0,1:T(8,128)} %param.42) | copy-start | bytes 6148
  180.4 143.6 %copy-start.14 = (f32[2048]{0:T(1024)S(1)}, f32[2048]{0:T(1024)}, u32[]{:S(2)}) copy-start(f32[2048]{0:T(1024)} %param.26) | copy-start | bytes 24580
  324.0 0.7 copy-start.5
  336.8 125.2 %copy-start.15 = (bf16[2,2048,64]{1,2,0:T(8,128)(2,1)S(1)}, bf16[2,2048,64]{1,2,0:T(8,128)(2,1)}, u32[]{:S(2)}) copy-start(bf16[2,2048,64]{1,2,0:T(8,128)(2,1)} %param.32) | copy-start | bytes 1572868
  473.1 116.7 %all-to-all-start.1 = ((bf16[32,2,9,2048]{3,1,2,0:T(2,128)(2,1)}), bf16[32,2,9,2048]{3,1,2,0:T(2,128)(2,1)S(1)}, u32[]{:S(2)}, u32[]{:S(2)}) async-start(bf16[32,2,9,2048]{3,1,2,0:T(2,128)(2,1)} %copy.70), calls=%async_computation.1 | async-start | bytes 4718592 | tf_op jit(solution)/shard_map/all_to_all | solution.py:191
  477.2 203.9 %reduce-scatter.2.cloned.1.call-start = ((), (), s32[]{:S(2)}) async-start(), calls=%async_computation.4 | async-start | bytes 557056 | tf_op jit(solution)/shard_map/reduce_scatter | solution.py:196
  599.9 5.1 copy-start.3
  606.0 76.5 %copy-start.4 = (bf16[1024,128]{1,0:T(8,128)(2,1)}, bf16[1024,128]{1,0:T(8,128)(2,1)S(1)}, u32[]{:S(2)}) copy-start(bf16[1024,128]{1,0:T(8,128)(2,1)S(1)} %scatter_fusion) | copy-start | bytes 786436
  606.9 75.6 %copy-start.1 = (bf16[1024,128]{1,0:T(8,128)(2,1)}, bf16[1024,128]{1,0:T(8,128)(2,1)S(1)}, u32[]{:S(2)}) copy-start(bf16[1024,128]{1,0:T(8,128)(2,1)S(1)} %scatter_fusion.1) | copy-start | bytes 786436
Sparse Core Ops, SparseCore 0:
  210.5 112.1 all-reduce.2
  604.3 76.7 reduce-scatter.1
where the time goes:
time: 690 us; the launch traced here: 689 us
  blocking collectives  308 us (45%)
  waiting for transfers between devices  295 us (43%)
  local copies, waits for them, and re-layouts  39.5 us (6%)
  between operations  17.8 us (3%)
  other arithmetic  12.3 us (2%)
  matrix products  12.3 us (2%)
    all_to_all x1, blocking collectives, body(): lax.all_to_all(send_rows, 'wide', split_axis=0, concat_axis=0, tiled=True)  125 us
    all_to_all x1, waiting for transfers between devices, body(): lax.all_to_all(produced, 'wide', split_axis=0, concat_axis=0, tiled=True)  111 us
    psum x1, waiting for transfers between devices, body(): summed = lax.psum(partial_value, 'narrow')  110 us
    reduce_scatter x1, waiting for transfers between devices, body(): lax.psum_scatter(partial_moe, 'narrow', scatter_dimension=1, tiled=True)  74.2 us
    all_gather x1, blocking collectives, body(): lax.all_gather(prefix_values, 'wide', axis=0, tiled=True)  37.7 us
    all_gather x1, blocking collectives, body(): lax.all_gather(query_weight, 'wide', axis=0, tiled=True)  30 us
    all_gather x1, blocking collectives, body(): lax.all_gather(value_weight, 'wide', axis=0, tiled=True)  29.9 us
    all_gather x1, blocking collectives, body(): lax.all_gather(output_weight, 'wide', axis=0, tiled=True)  28.5 us
  transfers between devices with their start and end apart: 3, of which 3 were waited for; matrix products, arithmetic and copies ran while one was open for 1% of the time, Pallas kernels for 0%

commit v1 on v0

--- a/solution.py
+++ b/solution.py
@@ -10,6 +10,15 @@
 WIN = 512
 CAP = 9
 norm_eps = 1e-06
+
+
+def added_up(array, name):
+    devices = lax.axis_size(name)
+    total, stride = (array, 1)
+    while stride < devices:
+        total = total + lax.ppermute(total, name, [(i, i ^ stride) for i in range(devices)])
+        stride = 2 * stride
+    return total
 
 
 def rms_scale(rows, row_gain):
@@ -160,7 +169,7 @@
     partial_value = lax.dot_general(
         attended, output_full, (((1,), (1,)), ((), ())), preferred_element_type=jnp.float32
     )
-    summed = lax.psum(partial_value, "narrow")
+    summed = added_up(partial_value, "narrow")
     mixed = (hidden.astype(jnp.float32) + summed).astype(jnp.bfloat16)
     mixed_part = lax.dynamic_slice_in_dim(mixed, narrow_pos * slice_width, slice_width, 1)
     normed_moe = rms_scale(mixed, expert_gain)

time: 690 us -> 635 us (0.920)
  waiting for transfers between devices: 295 us -> 231 us
  starting transfers between devices: 4.36 us -> 19.4 us
    psum x1 -> x0, waiting for transfers between devices: 110 us -> none  [body(): summed = lax.psum(partial_value, 'narrow')]
    ppermute x0 -> x4, waiting for transfers between devices: none -> 44.9 us  [added_up(): lax.ppermute(total, name, [(i, i ^ stride) for i in range(devices)])]
    ppermute x0 -> x4, starting transfers between devices: none -> 15 us  [added_up(): lax.ppermute(total, name, [(i, i ^ stride) for i in range(devices)])]
  transfers between devices with their start and end apart: 3 -> 6, of which waited for: 3 -> 6; matrix products, arithmetic and copies ran while one was open for 1% -> 1% of each run, Pallas kernels for 0% -> 0%
where the time goes in v1:
time: 635 us; the launch traced here: 634 us
  blocking collectives  303 us (48%)
  waiting for transfers between devices  231 us (36%)
  local copies, waits for them, and re-layouts  39.5 us (6%)
  starting transfers between devices  19.4 us (3%)
  between operations  17.8 us (3%)
  matrix products  11.5 us (2%)
  other arithmetic  11.4 us (2%)
    all_to_all x1, blocking collectives, body(): lax.all_to_all(send_rows, 'wide', split_axis=0, concat_axis=0, tiled=True)  120 us
    all_to_all x1, waiting for transfers between devices, body(): lax.all_to_all(produced, 'wide', split_axis=0, concat_axis=0, tiled=True)  111 us
    reduce_scatter x1, waiting for transfers between devices, body(): lax.psum_scatter(partial_moe, 'narrow', scatter_dimension=1, tiled=True)  75.9 us
    ppermute x4, waiting for transfers between devices, added_up(): lax.ppermute(total, name, [(i, i ^ stride) for i in range(devices)])  44.9 us
    all_gather x1, blocking collectives, body(): lax.all_gather(prefix_values, 'wide', axis=0, tiled=True)  37.7 us
    all_gather x1, blocking collectives, body(): lax.all_gather(query_weight, 'wide', axis=0, tiled=True)  30 us
    all_gather x1, blocking collectives, body(): lax.all_gather(value_weight, 'wide', axis=0, tiled=True)  29.9 us
    all_gather x1, blocking collectives, body(): lax.all_gather(output_weight, 'wide', axis=0, tiled=True)  28.5 us
  transfers between devices with their start and end apart: 6, of which 6 were waited for; matrix products, arithmetic and copies ran while one was open for 1% of the time, Pallas kernels for 0%

profile of v1, /device:TPU:2, one launch (start us, length us, event | category | flops | bytes accessed | tf_op | source)
XLA Modules:
  0.0 634.2 jit_solution(5509530451766584498)
XLA Ops:
  9.9 1.2 dynamic_slice.6
  15.9 1.4 gather_fusion.1
  23.1 37.7 %all_gather.18 = bf16[256,8,128]{2,0,1:T(8,128)(2,1)S(1)} all-gather(bf16[8,8,128]{2,0,1:T(8,128)(2,1)S(1)} %copy.59), channel_id=1, replica_groups=mesh['wide'=32,'narrow'=16] {'wide'}, dimensions={0}, use_global_device_ids=true | all-gather | bytes 540672 | tf_op jit(solution)/shard_map/all_gather | solution.py:92
  60.7 28.5 %all_gather.20 = bf16[256,8,128]{2,0,1:T(8,128)(2,1)S(1)} all-gather(bf16[8,8,128]{2,0,1:T(8,128)(2,1)S(1)} %copy.60), channel_id=1, replica_groups=mesh['wide'=32,'narrow'=16] {'wide'}, dimensions={0}, use_global_device_ids=true | all-gather | bytes 540672 | tf_op jit(solution)/shard_map/all_gather | solution.py:91
  89.2 30.0 %all_gather.19 = bf16[2048,128]{1,0:T(8,128)(2,1)S(1)} all-gather(bf16[64,128]{1,0:T(8,128)(2,1)S(1)} %copy-done.7), channel_id=1, replica_groups=mesh['wide'=32,'narrow'=16] {'wide'}, dimensions={0}, use_global_device_ids=true | all-gather | bytes 540672 | tf_op jit(solution)/shard_map/all_gather | solution.py:87
  119.2 28.5 %all_gather.21 = bf16[2048,128]{1,0:T(8,128)(2,1)S(1)} all-gather(bf16[64,128]{1,0:T(8,128)(2,1)S(1)} %copy-done.8), channel_id=1, replica_groups=mesh['wide'=32,'narrow'=16] {'wide'}, dimensions={0}, use_global_device_ids=true | all-gather | bytes 540672 | tf_op jit(solution)/shard_map/all_gather | solution.py:88
  150.2 29.9 %all_gather.22 = bf16[2048,128]{1,0:T(8,128)(2,1)S(1)} all-gather(bf16[64,128]{1,0:T(8,128)(2,1)S(1)} %copy-done.9), channel_id=1, replica_groups=mesh['wide'=32,'narrow'=16] {'wide'}, dimensions={0}, use_global_device_ids=true | all-gather | bytes 540672 | tf_op jit(solution)/shard_map/all_gather | solution.py:89
  180.3 28.5 %all_gather.23 = bf16[2048,128]{1,0:T(8,128)(2,1)S(1)} all-gather(bf16[64,128]{1,0:T(8,128)(2,1)S(1)} %copy-done.10), channel_id=1, replica_groups=mesh['wide'=32,'narrow'=16] {'wide'}, dimensions={0}, use_global_device_ids=true | all-gather | bytes 540672 | tf_op jit(solution)/shard_map/all_gather | solution.py:90
  209.6 2.4 collective-permute-start
  212.0 13.6 %collective-permute-done = f32[64,2048]{1,0:T(8,128)S(1)} collective-permute-done((f32[64,2048]{1,0:T(8,128)S(1)}, f32[64,2048]{1,0:T(8,128)S(1)}, u32[]{:S(2)}, u32[]{:S(2)}) %collective-permute-start) | collective-permute-done | bytes 524320 | tf_op jit(solution)/shard_map/ppermute | solution.py:19
  225.7 4.0 collective-permute-start.1
  229.7 12.7 %collective-permute-done.1 = f32[64,2048]{1,0:T(8,128)S(1)} collective-permute-done((f32[64,2048]{1,0:T(8,128)S(1)}, f32[64,2048]{1,0:T(8,128)S(1)}, u32[]{:S(2)}, u32[]{:S(2)}) %collective-permute-start.1) | collective-permute-done | bytes 524320 | tf_op jit(solution)/shard_map/ppermute | solution.py:19
  242.5 3.5 collective-permute-start.2
  246.2 10.7 %collective-permute-done.2 = f32[64,2048]{1,0:T(8,128)S(1)} collective-permute-done((f32[64,2048]{1,0:T(8,128)S(1)}, f32[64,2048]{1,0:T(8,128)S(1)}, u32[]{:S(2)}, u32[]{:S(2)}) %collective-permute-start.2) | collective-permute-done | bytes 524320 | tf_op jit(solution)/shard_map/ppermute | solution.py:19
  256.9 5.1 collective-permute-start.3
  262.3 1.2 reduce-window.6
  264.0 7.9 %collective-permute-done.3 = f32[64,2048]{1,0:T(8,128)S(1)} collective-permute-done((f32[64,2048]{1,0:T(8,128)S(1)}, f32[64,2048]{1,0:T(8,128)S(1)}, u32[]{:S(2)}, u32[]{:S(2)}) %collective-permute-start.3) | collective-permute-done | bytes 524320 | tf_op jit(solution)/shard_map/ppermute | solution.py:19
  272.8 4.5 scatter_custom_fusion
  277.3 2.8 reshape.738
  280.1 4.8 copy.67
  284.9 120.2 %all_to_all.10 = bf16[32,2,9,2048]{3,1,2,0:T(2,128)(2,1)S(1)} all-to-all(bf16[32,2,9,2048]{3,1,2,0:T(2,128)(2,1)S(1)} %copy.67), channel_id=1, replica_groups=mesh['wide'=32,'narrow'=16] {'wide'}, dimensions={0} | all-to-all | bytes 4718592 | tf_op jit(solution)/shard_map/all_to_all | solution.py:193
  405.2 1.6 fusion.9
  406.7 4.1 fusion.1
  410.8 5.5 copy.70
  416.3 4.1 all-to-all-start.1
  422.4 110.6 %all-to-all-done.1 = bf16[32,2,9,2048]{3,1,2,0:T(2,128)(2,1)S(1)} async-done(((bf16[32,2,9,2048]{3,1,2,0:T(2,128)(2,1)}), bf16[32,2,9,2048]{3,1,2,0:T(2,128)(2,1)S(1)}, u32[]{:S(2)}, u32[]{:S(2)}) %all-to-all-start.1) | async-done | bytes 2359328 | tf_op jit(solution)/shard_map/all_to_all | solution.py:200
  533.0 3.3 copy.71
  536.3 3.4 reshape.739
  539.7 3.3 gather_fusion
  543.1 4.2 fusion
  550.1 75.9 %reduce-scatter.2.cloned.1.call-done = f32[64,128]{1,0:T(8,128)} async-done(((f32[64,2048]{1,0:T(8,128)}), f32[64,128]{1,0:T(8,128)}) %reduce-scatter.2.cloned.1.call-update) | async-done | bytes 32784 | tf_op jit(solution)/shard_map/reduce_scatter | solution.py:205
  626.0 1.4 add_convert_fusion
  (112 shorter events, 19.9 us)
Async XLA Ops:
  7.2 399.6 %copy-start = (bf16[2,64,2048]{2,1,0:T(8,128)(2,1)S(1)}, bf16[2,64,2048]{2,1,0:T(8,128)(2,1)}, u32[]{:S(2)}) copy-start(bf16[2,64,2048]{2,1,0:T(8,128)(2,1)} %param.34) | copy-start | bytes 1572868
  8.2 140.2 %copy-start.2 = (bf16[1,1024,128]{2,1,0:T(8,128)(2,1)}, bf16[1,1024,128]{2,1,0:T(8,128)(2,1)S(1)}, u32[]{:S(2)}) copy-start(bf16[1,1024,128]{2,1,0:T(8,128)(2,1)S(1)} %copy.119) | copy-start | bytes 786436
  8.2 14.8 %copy-start.12 = (bf16[8,8,128]{2,1,0:T(8,128)(2,1)S(1)}, bf16[8,8,128]{2,1,0:T(8,128)(2,1)}, u32[]{:S(2)}) copy-start(bf16[8,8,128]{2,1,0:T(8,128)(2,1)} %param.35) | copy-start | bytes 49156
  8.2 14.8 %copy-start.13 = (bf16[8,8,128]{2,1,0:T(8,128)(2,1)S(1)}, bf16[8,8,128]{2,1,0:T(8,128)(2,1)}, u32[]{:S(2)}) copy-start(bf16[8,8,128]{2,1,0:T(8,128)(2,1)} %param.36) | copy-start | bytes 49156
  15.9 73.4 %copy-start.7 = (bf16[64,128]{1,0:T(8,128)(2,1)S(1)}, bf16[64,128]{1,0:T(8,128)(2,1)}, u32[]{:S(2)}) copy-start(bf16[64,128]{1,0:T(8,128)(2,1)} %param.27) | copy-start | bytes 49156
  18.0 101.2 %copy-start.8 = (bf16[64,128]{1,0:T(8,128)(2,1)S(1)}, bf16[64,128]{1,0:T(8,128)(2,1)}, u32[]{:S(2)}) copy-start(bf16[64,128]{1,0:T(8,128)(2,1)} %param.28) | copy-start | bytes 49156
  18.8 128.9 %copy-start.6 = (bf16[64,2048]{1,0:T(8,128)(2,1)S(1)}, bf16[64,2048]{1,0:T(8,128)(2,1)}, u32[]{:S(2)}) copy-start(bf16[64,2048]{1,0:T(8,128)(2,1)} %param.24) | copy-start | bytes 786436
  18.8 128.9 %copy-start.16 = (f32[2048]{0:T(1024)S(1)}, f32[2048]{0:T(1024)}, u32[]{:S(2)}) copy-start(f32[2048]{0:T(1024)} %param.25) | copy-start | bytes 24580
  89.2 61.0 %copy-start.9 = (bf16[64,128]{1,0:T(8,128)(2,1)S(1)}, bf16[64,128]{1,0:T(8,128)(2,1)}, u32[]{:S(2)}) copy-start(bf16[64,128]{1,0:T(8,128)(2,1)} %param.29) | copy-start | bytes 49156
  147.7 32.6 %copy-start.10 = (bf16[64,128]{1,0:T(8,128)(2,1)S(1)}, bf16[64,128]{1,0:T(8,128)(2,1)}, u32[]{:S(2)}) copy-start(bf16[64,128]{1,0:T(8,128)(2,1)} %param.30) | copy-start | bytes 49156
  208.9 37.2 %copy-start.11 = (s32[64,8]{0,1:T(8,128)S(1)}, s32[64,8]{0,1:T(8,128)}, u32[]{:S(2)}) copy-start(s32[64,8]{0,1:T(8,128)} %param.42) | copy-start | bytes 6148
  209.6 16.1 %collective-permute-start = (f32[64,2048]{1,0:T(8,128)S(1)}, f32[64,2048]{1,0:T(8,128)S(1)}, u32[]{:S(2)}, u32[]{:S(2)}) collective-permute-start(f32[64,2048]{1,0:T(8,128)S(1)} %fusion.35), channel_id=1, source_target_pairs={{0,1},{1,0},{2,3},{3,2},{4,5},{5,4},{6,7},{7,6},{8,9},{9,8},{10,11... | collective-permute-start | bytes 1572872 | tf_op jit(solution)/shard_map/ppermute | solution.py:19
  225.7 16.8 %collective-permute-start.1 = (f32[64,2048]{1,0:T(8,128)S(1)}, f32[64,2048]{1,0:T(8,128)S(1)}, u32[]{:S(2)}, u32[]{:S(2)}) collective-permute-start(f32[64,2048]{1,0:T(8,128)S(1)} %add.165), channel_id=1, source_target_pairs={{0,2},{1,3},{2,0},{3,1},{4,6},{5,7},{6,4},{7,5},{8,10},{9,11},{10,... | collective-permute-start | bytes 1572872 | tf_op jit(solution)/shard_map/ppermute | solution.py:19
  242.5 29.6 %copy-start.14 = (f32[2048]{0:T(1024)S(1)}, f32[2048]{0:T(1024)}, u32[]{:S(2)}) copy-start(f32[2048]{0:T(1024)} %param.26) | copy-start | bytes 24580
  242.5 14.3 %collective-permute-start.2 = (f32[64,2048]{1,0:T(8,128)S(1)}, f32[64,2048]{1,0:T(8,128)S(1)}, u32[]{:S(2)}, u32[]{:S(2)}) collective-permute-start(f32[64,2048]{1,0:T(8,128)S(1)} %add.166), channel_id=1, source_target_pairs={{0,4},{1,5},{2,6},{3,7},{4,0},{5,1},{6,2},{7,3},{8,12},{9,13},{10,... | collective-permute-start | bytes 1572872 | tf_op jit(solution)/shard_map/ppermute | solution.py:19
  256.9 14.9 %collective-permute-start.3 = (f32[64,2048]{1,0:T(8,128)S(1)}, f32[64,2048]{1,0:T(8,128)S(1)}, u32[]{:S(2)}, u32[]{:S(2)}) collective-permute-start(f32[64,2048]{1,0:T(8,128)S(1)} %add.167), channel_id=1, source_target_pairs={{0,8},{1,9},{2,10},{3,11},{4,12},{5,13},{6,14},{7,15},{8,0},{9,1},... | collective-permute-start | bytes 1572872 | tf_op jit(solution)/shard_map/ppermute | solution.py:19
  272.1 0.7 copy-start.5
  284.9 120.2 %copy-start.15 = (bf16[2,2048,64]{1,2,0:T(8,128)(2,1)S(1)}, bf16[2,2048,64]{1,2,0:T(8,128)(2,1)}, u32[]{:S(2)}) copy-start(bf16[2,2048,64]{1,2,0:T(8,128)(2,1)} %param.32) | copy-start | bytes 1572868
  416.3 116.7 %all-to-all-start.1 = ((bf16[32,2,9,2048]{3,1,2,0:T(2,128)(2,1)}), bf16[32,2,9,2048]{3,1,2,0:T(2,128)(2,1)S(1)}, u32[]{:S(2)}, u32[]{:S(2)}) async-start(bf16[32,2,9,2048]{3,1,2,0:T(2,128)(2,1)} %copy.70), calls=%async_computation.1 | async-start | bytes 4718592 | tf_op jit(solution)/shard_map/all_to_all | solution.py:200
  420.3 205.7 %reduce-scatter.2.cloned.1.call-start = ((), (), s32[]{:S(2)}) async-start(), calls=%async_computation.3 | async-start | bytes 557056 | tf_op jit(solution)/shard_map/reduce_scatter | solution.py:205
  543.1 5.1 copy-start.3
  549.1 78.3 %copy-start.4 = (bf16[1024,128]{1,0:T(8,128)(2,1)}, bf16[1024,128]{1,0:T(8,128)(2,1)S(1)}, u32[]{:S(2)}) copy-start(bf16[1024,128]{1,0:T(8,128)(2,1)S(1)} %scatter_fusion) | copy-start | bytes 786436
  550.1 77.3 %copy-start.1 = (bf16[1024,128]{1,0:T(8,128)(2,1)}, bf16[1024,128]{1,0:T(8,128)(2,1)S(1)}, u32[]{:S(2)}) copy-start(bf16[1024,128]{1,0:T(8,128)(2,1)S(1)} %scatter_fusion.1) | copy-start | bytes 786436
Sparse Core Ops, SparseCore 0:
  547.5 78.5 reduce-scatter.1
